TPU v7x, 32 devices: a whole 2x2x4 slice. The times are simulated.
32 devices in a mesh: batch: 8 (over y, x, core), mp: 4 (over z).
Axes of the slice: x: 2, y: 2, z: 4, core: 2. Of those that a mesh axis runs over, the one named last changes fastest.
Arguments:
- token_ids: int32 [8, 1536], P('batch'), may hold values from 0 to 30527
- segment_ids: int32 [8, 1536], P('batch'), may hold values from 0 to 8, never falling along the last dimension, each value on 1 to 1024 neighbouring positions
- row_of: int32 [30528], replicated, may hold values from 0 to 30527, each once
- query_count: int32 [1], replicated, may hold values from 16 to 32
- table: float32 [30528, 768], P('batch'), may hold values from -8 to 8
- qkv_weight: float32 [768, 3, 768], P('batch', None, 'mp'), may hold values from -0.21875 to 0.21875
- out_weight: float32 [768, 768], P('mp', 'batch'), may hold values from -0.875 to 0.875
- gate_up_weight: float32 [768, 2, 3072], P('batch', None, 'mp'), may hold values from -0.21875 to 0.21875
- down_weight: float32 [3072, 768], P('mp', 'batch'), may hold values from -0.109375 to 0.109375
- gains: float32 [2, 768], P(None, 'batch'), may hold values from 0.3 to 2.5
- table_m: float32 [30528, 768], P('batch'), may hold values from -0.0009765625 to 0.0009765625
- qkv_m: float32 [768, 3, 768], P('batch', None, 'mp'), may hold values from -0.0009765625 to 0.0009765625
- out_m: float32 [768, 768], P('mp', 'batch'), may hold values from -0.0009765625 to 0.0009765625
- gate_up_m: float32 [768, 2, 3072], P('batch', None, 'mp'), may hold values from -0.0009765625 to 0.0009765625
- down_m: float32 [3072, 768], P('mp', 'batch'), may hold values from -0.0009765625 to 0.0009765625
- gains_m: float32 [2, 768], P(None, 'batch'), may hold values from -0.0009765625 to 0.0009765625
- table_v: float32 [30528, 768], P('batch'), may hold values from 3.040972e-08 to 1.2163888e-07
- qkv_v: float32 [768, 3, 768], P('batch', None, 'mp'), may hold values from 3.040972e-08 to 1.2163888e-07
- out_v: float32 [768, 768], P('mp', 'batch'), may hold values from 3.040972e-08 to 1.2163888e-07
- gate_up_v: float32 [768, 2, 3072], P('batch', None, 'mp'), may hold values from 3.040972e-08 to 1.2163888e-07
- down_v: float32 [3072, 768], P('mp', 'batch'), may hold values from 3.040972e-08 to 1.2163888e-07
- gains_v: float32 [2, 768], P(None, 'batch'), may hold values from 3.040972e-08 to 1.2163888e-07
Outputs:
- loss: float32 [1], replicated
- grad_norm: float32 [1], replicated
- new_table: float32 [30528, 768], P('batch')
- new_qkv_weight: float32 [768, 3, 768], P('batch', None, 'mp')
- new_out_weight: float32 [768, 768], P('mp', 'batch')
- new_gate_up_weight: float32 [768, 2, 3072], P('batch', None, 'mp')
- new_down_weight: float32 [3072, 768], P('mp', 'batch')
- new_gains: float32 [2, 768], P(None, 'batch')
- clipped_table_grad: float32 [30528, 768], P('batch')
- new_qkv_m: float32 [768, 3, 768], P('batch', None, 'mp')
- new_out_m: float32 [768, 768], P('mp', 'batch')
- new_gate_up_m: float32 [768, 2, 3072], P('batch', None, 'mp')
- new_down_m: float32 [3072, 768], P('mp', 'batch')
- new_gains_m: float32 [2, 768], P(None, 'batch')
- new_table_v: float32 [30528, 768], P('batch')
- new_qkv_v: float32 [768, 3, 768], P('batch', None, 'mp')
- new_out_v: float32 [768, 768], P('mp', 'batch')
- new_gate_up_v: float32 [768, 2, 3072], P('batch', None, 'mp')
- new_down_v: float32 [3072, 768], P('mp', 'batch')
- new_gains_v: float32 [2, 768], P(None, 'batch')
Inputs may be any that keep to these rules, and one draw needn't show every extreme that they name: `segment_ids`: in each row the ids never fall, every id 0 to 8 appears, id 8 marks padding, each segment has 1 to 1024 tokens and one has exactly 1024. A permutation: token t's embedding is table row row_of[t]. The first query_count queries count.
All inputs are finite; a program needn't handle non-finite values.
Results may differ from a plain program's by a relative error of at most 0.0075.
The roundings to bfloat16 on the way count: a program that leaves them out, or rounds other values in their place, can miss the bound.
Values may be sent and summed in bfloat16 or wider, within the bound.
A program may use at most 320 MiB of HBM per device.

v0:
```python
from functools import partial
import jax
import jax.numpy as jnp
from jax import lax
from jax.sharding import PartitionSpec as P

D = 768
HEAD_DIM = 64
SEGS = 8
peak_affinity = lax.Precision.HIGHEST
sharpness_divisor = 0.05
clip_limit = 1.0
step_number = 3.0
rates = (0.3, 0.02, 0.02, 0.02, 0.02, 0.3)
negative = -1e30


def positions(segment_row, segment_count):
    labels = jnp.arange(segment_count + 1, dtype=jnp.int32)
    member = (segment_row[:, None] == labels[None, :]).astype(jnp.int32)
    counts = jnp.sum(member, 0)
    starts = jnp.cumsum(counts) - counts
    first_index = jnp.sum(member * starts[None, :], 1)
    return (jnp.arange(segment_row.shape[0], dtype=jnp.int32) - first_index).astype(jnp.float32)


def rotate(values, places):
    half_dim = values.shape[-1] // 2
    freqs = jnp.power(1000.0, -2.0 * jnp.arange(half_dim, dtype=jnp.float32) / values.shape[-1])
    angles = places[:, None] * freqs[None, :]
    cosine = jnp.cos(angles)[:, None, :]
    sine = jnp.sin(angles)[:, None, :]
    former = values[..., :half_dim]
    latter = values[..., half_dim:]
    return jnp.concatenate([former * cosine - latter * sine, latter * cosine + former * sine], -1)


def layer_norm(values, gain):
    centred = values - jnp.mean(values, -1, keepdims=True)
    spread = jnp.mean(centred * centred, -1, keepdims=True)
    return centred * lax.rsqrt(spread + 1e-05) * gain


def swiglu(gate_up):
    return jax.nn.silu(gate_up[:, 0]) * gate_up[:, 1]


def contract(left, right, left_dim, right_dim):
    return lax.dot_general(
        left, right, (((left_dim,), (right_dim,)), ((), ())), preferred_element_type=jnp.float32
    )


def pool_rows(hidden, segment_ids):
    rows_dev, length = segment_ids.shape
    labels = jnp.arange(SEGS, dtype=jnp.int32)
    member = (segment_ids[:, None, :] == labels[None, :, None]).astype(jnp.float32)
    sums = jnp.einsum(
        "rsl,rld->rsd", member, hidden.reshape(rows_dev, length, -1), precision=peak_affinity
    )
    pooled = (sums / jnp.sum(member, -1, keepdims=True)).reshape(rows_dev * SEGS, -1)
    return pooled * lax.rsqrt(jnp.sum(pooled * pooled, -1, keepdims=True) + 1e-06)


def block_scores(query_block, key_row, segment_block, segment_row):
    scores = jnp.einsum(
        "qhd,khd->hqk", query_block, key_row, preferred_element_type=jnp.float32
    ) * HEAD_DIM ** (-0.5)
    same = segment_block[:, None] == segment_row[None, :]
    return jnp.where(same[None], scores, negative)


def attend(query, keys, values, segment_ids, width):
    rows_dev, length = segment_ids.shape
    per_row = length // width
    flat_segments = segment_ids.reshape(-1)

    def one_block(block):
        row_index = block // per_row
        query_block = lax.dynamic_slice_in_dim(query, block * width, width, 0)
        segment_block = lax.dynamic_slice_in_dim(flat_segments, block * width, width, 0)
        scores = block_scores(query_block, keys[row_index], segment_block, segment_ids[row_index])
        peak_score = jnp.max(scores, -1, keepdims=True)
        weights = jnp.exp(scores - peak_score)
        totals = jnp.sum(weights, -1, keepdims=True)
        probs = (weights / totals).astype(jnp.bfloat16)
        output = jnp.einsum(
            "hqk,khd->qhd", probs, values[row_index], preferred_element_type=jnp.float32
        )
        return (output, (peak_score + jnp.log(totals))[..., 0])

    outputs, log_totals = lax.map(one_block, jnp.arange(rows_dev * per_row, dtype=jnp.int32))
    return (outputs.reshape((rows_dev * length,) + outputs.shape[2:]), log_totals)


def attend_back(query, keys, values, segment_ids, log_totals, grad_out, width):
    rows_dev, length = segment_ids.shape
    per_row = length // width
    flat_segments = segment_ids.reshape(-1)
    factor = HEAD_DIM ** (-0.5)

    def one_block(carry, block):
        grad_keys, grad_values = carry
        row_index = block // per_row
        query_block = lax.dynamic_slice_in_dim(query, block * width, width, 0)
        segment_block = lax.dynamic_slice_in_dim(flat_segments, block * width, width, 0)
        grad_block = lax.dynamic_slice_in_dim(grad_out, block * width, width, 0)
        scores = block_scores(query_block, keys[row_index], segment_block, segment_ids[row_index])
        probs = jnp.exp(scores - log_totals[block][..., None])
        grad_probs = jnp.einsum(
            "qhd,khd->hqk", grad_block, values[row_index], preferred_element_type=jnp.float32
        )
        inner = jnp.sum(probs * grad_probs, -1, keepdims=True)
        grad_scores = (probs * (grad_probs - inner)).astype(jnp.bfloat16)
        grad_query = (
            jnp.einsum(
                "hqk,khd->qhd", grad_scores, keys[row_index], preferred_element_type=jnp.float32
            )
            * factor
        )
        key_term = (
            jnp.einsum("hqk,qhd->khd", grad_scores, query_block, preferred_element_type=jnp.float32)
            * factor
        )
        value_term = jnp.einsum(
            "hqk,qhd->khd",
            probs.astype(jnp.bfloat16),
            grad_block,
            preferred_element_type=jnp.float32,
        )
        return (
            (grad_keys.at[row_index].add(key_term), grad_values.at[row_index].add(value_term)),
            grad_query,
        )

    zeros = jnp.zeros(keys.shape, jnp.float32)
    (grad_keys, grad_values), grad_query = lax.scan(
        one_block, (zeros, zeros), jnp.arange(rows_dev * per_row, dtype=jnp.int32)
    )
    return (grad_query.reshape((rows_dev * length,) + grad_query.shape[2:]), grad_keys, grad_values)


def adam_update(weight, grad, first, second, rate):
    first = 0.5 * first + 0.5 * grad
    second = 0.5 * second + 0.5 * grad * grad
    correction = 1.0 - 0.5**step_number
    weight = weight - rate * (
        first / correction / (jnp.sqrt(second / correction) + 1e-08) + 0.01 * weight
    )
    return (weight, first, second)


def local(
    token_ids,
    segment_ids,
    row_of,
    query_count,
    table,
    qkv_weight,
    out_weight,
    gate_up_weight,
    down_weight,
    gains,
    table_m,
    qkv_m,
    out_m,
    gate_up_m,
    down_m,
    gains_m,
    table_v,
    qkv_v,
    out_v,
    gate_up_v,
    down_v,
    gains_v,
):
    local_width = table.shape[1] // lax.axis_size("mp")
    column = lax.axis_index("mp") * local_width
    table_cols = lax.dynamic_slice_in_dim(table, column, local_width, 1)
    low_table, w_qkv, w_out, w_gu, w_down, gain_low = (
        lax.all_gather(table_cols.astype(jnp.bfloat16), "batch", axis=0, tiled=True),
        lax.all_gather(qkv_weight.astype(jnp.bfloat16), "batch", axis=0, tiled=True),
        lax.all_gather(out_weight.astype(jnp.bfloat16), "batch", axis=1, tiled=True),
        lax.all_gather(gate_up_weight.astype(jnp.bfloat16), "batch", axis=0, tiled=True),
        lax.all_gather(down_weight.astype(jnp.bfloat16), "batch", axis=1, tiled=True),
        lax.all_gather(gains.astype(jnp.bfloat16), "batch", axis=1, tiled=True),
    )
    gain = gain_low.astype(jnp.float32)
    rows_dev, length = token_ids.shape
    tokens = rows_dev * length
    width = min(512, length)
    heads_local = w_qkv.shape[2] // HEAD_DIM
    ff_local = w_gu.shape[2]
    table_rows = row_of[token_ids.reshape(-1)]
    x_zero = lax.all_gather(low_table[table_rows], "mp", axis=1, tiled=True)
    places = jax.vmap(partial(positions, segment_count=SEGS))(segment_ids).reshape(-1)
    qkv = jnp.dot(x_zero, w_qkv.reshape(D, -1), preferred_element_type=jnp.float32).reshape(
        tokens, 3, heads_local, HEAD_DIM
    )
    query = rotate(qkv[:, 0], places).astype(jnp.bfloat16)
    keys = (
        rotate(qkv[:, 1], places)
        .astype(jnp.bfloat16)
        .reshape(rows_dev, length, heads_local, HEAD_DIM)
    )
    values = qkv[:, 2].astype(jnp.bfloat16).reshape(rows_dev, length, heads_local, HEAD_DIM)
    attended, log_totals = attend(query, keys, values, segment_ids, width)
    attended_low = attended.reshape(tokens, -1).astype(jnp.bfloat16)
    attn_term = jnp.dot(attended_low, w_out, preferred_element_type=jnp.float32)
    attn = lax.psum(attn_term, "mp")
    hidden_one, first_back = jax.vjp(layer_norm, x_zero.astype(jnp.float32) + attn, gain[0])
    hidden_low = hidden_one.astype(jnp.bfloat16)
    gate_up = jnp.dot(hidden_low, w_gu.reshape(D, -1), preferred_element_type=jnp.float32).reshape(
        tokens, 2, ff_local
    )
    active, swiglu_back = jax.vjp(swiglu, gate_up)
    active_low = active.astype(jnp.bfloat16)
    mlp = lax.psum(jnp.dot(active_low, w_down, preferred_element_type=jnp.float32), "mp")
    hidden_two, second_back = jax.vjp(layer_norm, hidden_one + mlp, gain[1])
    embed, pool_back = jax.vjp(lambda hidden: pool_rows(hidden, segment_ids), hidden_two)
    batch_index = lax.axis_index("batch")
    half_count = lax.axis_size("batch") // 2
    texts = embed.shape[0]
    queries_all = half_count * texts
    everyone = lax.all_gather(embed, "batch", axis=0, tiled=True)
    question_vectors = everyone[:queries_all]
    passage_vectors = everyone[queries_all:]
    limit = query_count[0].astype(jnp.float32)
    labels = jnp.arange(queries_all, dtype=jnp.int32)
    weight_rows = (labels < query_count[0]).astype(jnp.float32) / limit
    affinity_scores = (
        jnp.dot(question_vectors, passage_vectors.T, precision=peak_affinity) / sharpness_divisor
    )
    target = (labels[:, None] == labels[None, :]).astype(jnp.float32)
    loss_value = jnp.sum(
        weight_rows
        * (jax.nn.logsumexp(affinity_scores, -1) - jnp.sum(affinity_scores * target, -1))
    )
    affinity_derivative = (jax.nn.softmax(affinity_scores, -1) - target) * weight_rows[:, None]
    grad_all = jnp.concatenate(
        [
            jnp.dot(affinity_derivative, passage_vectors, precision=peak_affinity)
            / sharpness_divisor,
            jnp.dot(affinity_derivative.T, question_vectors, precision=peak_affinity)
            / sharpness_divisor,
        ],
        0,
    )
    grad_embed = lax.dynamic_slice_in_dim(grad_all, batch_index * texts, texts, 0)
    (grad_two,) = pool_back(grad_embed)
    grad_second, grad_gain_two = second_back(grad_two)
    grad_mlp_low = grad_second.astype(jnp.bfloat16)
    grad_active = contract(grad_mlp_low, w_down, 1, 1)
    grad_down = contract(active_low, grad_mlp_low, 0, 0)
    (grad_gate_up,) = swiglu_back(grad_active)
    grad_gu_low = grad_gate_up.reshape(tokens, -1).astype(jnp.bfloat16)
    back_term = contract(grad_gu_low, w_gu.reshape(D, -1), 1, 1)
    grad_one = grad_second + lax.psum(back_term, "mp")
    grad_first, grad_gain_one = first_back(grad_one)
    grad_gu = contract(hidden_low, grad_gu_low, 0, 0)
    grad_attn_low = grad_first.astype(jnp.bfloat16)
    grad_attended = contract(grad_attn_low, w_out, 1, 1).astype(jnp.bfloat16)
    grad_out = contract(attended_low, grad_attn_low, 0, 0)
    grad_query, grad_keys, grad_values = attend_back(
        query,
        keys,
        values,
        segment_ids,
        log_totals,
        grad_attended.reshape(tokens, heads_local, HEAD_DIM),
        width,
    )
    _, rotate_back = jax.vjp(lambda inputs: rotate(inputs, places), qkv[:, 0])
    (grad_query_raw,) = rotate_back(grad_query)
    (grad_key_raw,) = rotate_back(grad_keys.reshape(tokens, heads_local, HEAD_DIM))
    grad_qkv_low = (
        jnp.stack(
            [grad_query_raw, grad_key_raw, grad_values.reshape(tokens, heads_local, HEAD_DIM)], 1
        )
        .reshape(tokens, -1)
        .astype(jnp.bfloat16)
    )
    grad_zero = grad_first + lax.psum(contract(grad_qkv_low, w_qkv.reshape(D, -1), 1, 1), "mp")
    grad_qkv = contract(x_zero, grad_qkv_low, 0, 0)
    grad_table = (
        jnp.zeros((low_table.shape[0], local_width), jnp.float32)
        .at[table_rows]
        .add(lax.dynamic_slice_in_dim(grad_zero, column, local_width, 1))
    )
    grad_gains = jnp.stack([grad_gain_one, grad_gain_two], 0)
    reduced = (
        lax.psum_scatter(grad_table, "batch", scatter_dimension=0, tiled=True),
        lax.psum_scatter(grad_qkv.reshape(D, 3, -1), "batch", scatter_dimension=0, tiled=True),
        lax.psum_scatter(grad_out, "batch", scatter_dimension=1, tiled=True),
        lax.psum_scatter(grad_gu.reshape(D, 2, -1), "batch", scatter_dimension=0, tiled=True),
        lax.psum_scatter(grad_down, "batch", scatter_dimension=1, tiled=True),
        lax.psum_scatter(grad_gains, "batch", scatter_dimension=1, tiled=True),
    )
    squares = sum((jnp.sum(part * part) for part in reduced[:5])) + jnp.sum(
        reduced[5] * reduced[5]
    ) / lax.axis_size("mp")
    table_full = lax.all_gather(reduced[0], "mp", axis=1, tiled=True)
    total_squares = lax.psum(squares, ("batch", "mp"))
    grad_norm = jnp.sqrt(total_squares)
    scale = clip_limit / jnp.maximum(grad_norm, clip_limit)
    olds = (table, qkv_weight, out_weight, gate_up_weight, down_weight, gains)
    grads_all = (table_full,) + tuple(reduced[1:])
    firsts = (table_m, qkv_m, out_m, gate_up_m, down_m, gains_m)
    seconds = (table_v, qkv_v, out_v, gate_up_v, down_v, gains_v)
    updated = [
        adam_update(weight_old, grad_part * scale, first_old, second_old, rate)
        for weight_old, grad_part, first_old, second_old, rate in zip(
            olds, grads_all, firsts, seconds, rates
        )
    ]
    clipped_table = table_full * scale
    loss = loss_value.reshape(1)
    return (
        loss,
        grad_norm.reshape(1),
        updated[0][0],
        updated[1][0],
        updated[2][0],
        updated[3][0],
        updated[4][0],
        updated[5][0],
        clipped_table,
        updated[1][1],
        updated[2][1],
        updated[3][1],
        updated[4][1],
        updated[5][1],
        updated[0][2],
        updated[1][2],
        updated[2][2],
        updated[3][2],
        updated[4][2],
        updated[5][2],
    )


def solution(mesh):
    placed = (
        P("batch", None),
        P("batch", None),
        P(),
        P(),
        P("batch", None),
        P("batch", None, "mp"),
        P("mp", "batch"),
        P("batch", None, "mp"),
        P("mp", "batch"),
        P(None, "batch"),
        P("batch", None),
        P("batch", None, "mp"),
        P("mp", "batch"),
        P("batch", None, "mp"),
        P("mp", "batch"),
        P(None, "batch"),
        P("batch", None),
        P("batch", None, "mp"),
        P("mp", "batch"),
        P("batch", None, "mp"),
        P("mp", "batch"),
        P(None, "batch"),
    )
    return jax.shard_map(
        local,
        mesh=mesh,
        in_specs=placed,
        out_specs=(
            P(),
            P(),
            P("batch", None),
            P("batch", None, "mp"),
            P("mp", "batch"),
            P("batch", None, "mp"),
            P("mp", "batch"),
            P(None, "batch"),
            P("batch", None),
            P("batch", None, "mp"),
            P("mp", "batch"),
            P("batch", None, "mp"),
            P("mp", "batch"),
            P(None, "batch"),
            P("batch", None),
            P("batch", None, "mp"),
            P("mp", "batch"),
            P("batch", None, "mp"),
            P("mp", "batch"),
            P(None, "batch"),
        ),
        check_vma=False,
    )
```

profile of v0, /device:TPU:0, one launch (start us, length us, event | category | flops | bytes accessed | tf_op | source)
XLA Modules:
  0.0 1895.6 jit_solution(3074774490312549609)
XLA Ops:
  7.3 12.4 copy.141
  31.4 63.1 %all-gather.17.cloned.1.call-done = bf16[8,3816,192]{1,2,0:T(8,128)(2,1)} async-done(((bf16[1,3816,192]{1,2,0:T(8,128)(2,1)}), bf16[8,3816,192]{1,2,0:T(8,128)(2,1)}) %all-gather.17.cloned.1.call-update) | async-done | bytes 11722768 | tf_op jit(solution)/shard_map/all_gather | solution.py:181
  94.5 18.1 copy.142
  112.6 11.2 gather_fusion.1
  126.6 13.2 all_gather.29
  151.9 23.6 %all-gather.15.cloned.1.call-done = bf16[1536,768]{0,1:T(8,128)(2,1)} async-done(((bf16[1536,192]{0,1:T(8,128)(2,1)}), bf16[1536,768]{0,1:T(8,128)(2,1)}) %all-gather.15.cloned.1.call-update) | async-done | bytes 2359312 | tf_op jit(solution)/shard_map/all_gather | solution.py:195
  179.8 33.9 %while.31 = (s32[]{:T(128)}, bf16[3,512,3,64]{1,3,2,0:T(8,128)(2,1)}, f32[3,3,512]{2,1,0:T(4,128)S(1)}, s32[3]{0:T(128)S(1)}, s32[1536]{0:T(1024)S(1)}, /*index=...) while((s32[]{:T(128)}, ...), condition=%wide.region_6.7_spmd, body=%wide.region_3.6_spmd.sunk | while | flops 633076224 | bytes 38029568 | solution.py:92
  232.6 156.8 %all-reduce.11.cloned.1.call-done = f32[1536,768]{0,1:T(8,128)} async-done(((f32[1536,768]{0,1:T(8,128)}), f32[1536,768]{0,1:T(8,128)}) %all-reduce.11.cloned.1.call-update) | async-done | bytes 4718608 | tf_op jit(solution)/shard_map/psum | solution.py:210
  421.9 171.2 %all-reduce.13.cloned.1.call-done = f32[1536,768]{0,1:T(8,128)} async-done(((f32[1536,768]{0,1:T(8,128)}), f32[1536,768]{0,1:T(8,128)}) %all-reduce.13.cloned.1.call-update) | async-done | bytes 4718608 | tf_op jit(solution)/shard_map/psum | solution.py:218
  601.2 9.5 all_gather.34
  633.7 169.7 %all-reduce.15.cloned.1.call-done = f32[1536,768]{0,1:T(8,128)} async-done(((f32[1536,768]{0,1:T(8,128)}), f32[1536,768]{0,1:T(8,128)}) %all-reduce.15.cloned.1.call-update) | async-done | bytes 4718608 | tf_op jit(solution)/shard_map/psum | solution.py:258
  821.4 161.7 %while.32 = (s32[]{:T(128)}, f32[1,1536,3,64]{1,3,2,0:T(8,128)}, f32[1,1536,3,64]{1,3,2,0:T(8,128)S(1)}, f32[3,512,3,64]{1,0,3,2:T(4,128)}, s32[3]{0:T(128)S(1)}...) while((s32[]{:T(128)}, f32[1,1536,3,64]{1,3,2,0:T(8,128)}, ...), condition=%wide.region_29.30_spmd.clone, body=%wide.region_26.29_spmd.clone.sunk | while | flops 1534130688 | bytes 86367704 | solution.py:137
  839.3 9.4 multiply_convert_fusion.4
  893.0 9.4 multiply_convert_fusion.4
  993.0 171.1 %all-reduce.17.cloned.1.call-done = f32[1536,768]{0,1:T(8,128)} async-done(((f32[1536,768]{0,1:T(8,128)}), f32[1536,768]{0,1:T(8,128)}) %all-reduce.17.cloned.1.call-update) | async-done | bytes 4718608 | tf_op jit(solution)/shard_map/psum | solution.py:283
  1166.3 21.2 %scatter_custom_fusion = f32[30528,192]{1,0:T(8,128)} fusion(s32[1536]{0:T(1024)} %copy-done.49, f32[1536,192]{1,0:T(8,128)S(1)} %copy.157, f32[]{:T(128)} %constant.228.clone.1), kind=kCustom, calls=%fused_computation.51 | custom fusion | flops 294912 | bytes 23446016 | tf_op jit(solution)/shard_map/scatter-add | solution.py:288
  1201.7 15.3 fusion.50
  1224.7 151.4 %reduce-scatter.11.cloned.1.call-done = f32[3816,192]{1,0:T(8,128)} async-done(((f32[30528,192]{1,0:T(8,128)}), f32[3816,192]{1,0:T(8,128)}) %reduce-scatter.11.cloned.1.call-update) | async-done | bytes 2930704 | tf_op jit(solution)/shard_map/reduce_scatter | solution.py:292
  1381.2 12.6 copy.160
  1393.8 28.0 %reduce-scatter.17.cloned.1.call-done = f32[768,96]{0,1:T(8,128)} async-done(((f32[768,768]{0,1:T(8,128)}), f32[768,96]{0,1:T(8,128)}) %reduce-scatter.17.cloned.1.call-update) | async-done | bytes 294928 | tf_op jit(solution)/shard_map/reduce_scatter | solution.py:296
  1423.5 36.1 %reduce-scatter.21.cloned.1.call-done = f32[96,2]{1,0:T(8,128)} async-done(((f32[768,2]{1,0:T(8,128)}), f32[96,2]{1,0:T(8,128)}) %reduce-scatter.21.cloned.1.call-update) | async-done | bytes 784
  1461.8 36.2 %reduce-scatter.19.cloned.1.call-done = f32[96,192]{1,0:T(8,128)} async-done(((f32[768,192]{1,0:T(8,128)}), f32[96,192]{1,0:T(8,128)}) %reduce-scatter.19.cloned.1.call-update) | async-done | bytes 73744
  1499.6 56.7 %reduce-scatter.15.cloned.1.call-done = f32[96,2,768]{2,0,1:T(8,128)} async-done(((f32[768,2,768]{2,0,1:T(8,128)}), f32[96,2,768]{2,0,1:T(8,128)}) %reduce-scatter.15.cloned.1.call-update) | async-done | bytes 589840 | tf_op jit(solution)/shard_map/reduce_scatter | solution.py:295
  1558.1 44.5 %reduce-scatter.13.cloned.1.call-done = f32[96,3,192]{2,0,1:T(8,128)} async-done(((f32[768,3,192]{2,0,1:T(8,128)}), f32[96,3,192]{2,0,1:T(8,128)}) %reduce-scatter.13.cloned.1.call-update) | async-done | bytes 221200 | tf_op jit(solution)/shard_map/reduce_scatter | solution.py:293
  1611.3 13.3 copy.158
  1624.7 53.5 %psum.39 = f32[]{:T(128)} all-reduce(f32[]{:T(128)S(6)} %add.324), channel_id=1, replica_groups=mesh['batch'=8,'mp'=4] {'batch','mp'}, use_global_device_ids=true, to_apply=%region_46.47 | all-reduce | flops 1 | bytes 8 | tf_op jit(solution)/shard_map/psum | solution.py:303
  1687.7 123.4 %all-gather.13.cloned.1.call-done = f32[3816,768]{0,1:T(8,128)} async-done(((f32[3816,192]{0,1:T(8,128)}), f32[3816,768]{0,1:T(8,128)}) %all-gather.13.cloned.1.call-update) | async-done | bytes 11722768 | tf_op jit(solution)/shard_map/all_gather | solution.py:302
  1811.0 17.3 fusion.46
  1828.4 12.3 copy.169
  1840.7 22.2 %fusion.45 = f32[3816,768]{0,1:T(8,128)} fusion(f32[3816,768]{0,1:T(8,128)} %copy.141, f32[3816,768]{0,1:T(8,128)} %get-tuple-element.440, f32[3816,768]{0,1:T(8,128)} %copy.158, f32[3816,768]{0,1:T(8,128)} %copy.160), kind=kLoop, calls=%fused_computation.57 | loop fusion | flops 41029632 | bytes 58613760 | tf_op jit(solution)/shard_map/sub | solution.py:147
  1862.9 12.3 copy.167
  1875.3 12.4 copy.171
  (347 shorter events, 350.5 us)
Async XLA Ops:
  7.2 87.3 %all-gather.17.cloned.1.call-start = ((), (), s32[]{:S(2)}) async-start(), calls=%async_computation.18 | async-start | bytes 13271040 | tf_op jit(solution)/shard_map/all_gather | solution.py:181
  22.8 152.7 %all-gather.15.cloned.1.call-start = ((), (), s32[]{:S(2)}) async-start(), calls=%async_computation.17 | async-start | bytes 2949120 | tf_op jit(solution)/shard_map/all_gather | solution.py:195
  31.4 81.2 %copy-start.49 = (s32[1536]{0:T(1024)}, s32[1536]{0:T(1024)S(1)}, u32[]{:S(2)}) copy-start(s32[1536]{0:T(1024)S(1)} %fusion.104) | copy-start | bytes 18436
  124.8 103.5 %all-gather.9.cloned.1.call-start = ((), (), s32[]{:S(2)}) async-start(), calls=%async_computation.7 | async-start | bytes 2654208 | tf_op jit(solution)/shard_map/all_gather | solution.py:184
  125.7 263.7 %all-reduce.11.cloned.1.call-start = ((), (), s32[]{:S(2)}) async-start(), calls=%async_computation.6 | async-start | bytes 9437184 | tf_op jit(solution)/shard_map/psum | solution.py:210
  151.1 64.4 %copy-start.10 = (bf16[192,768]{0,1:T(8,128)(2,1)}, bf16[192,768]{0,1:T(8,128)(2,1)S(1)}, u32[]{:S(2)}) copy-start(bf16[192,768]{0,1:T(8,128)(2,1)S(1)} %all_gather.30) | copy-start | bytes 884740
  218.5 196.3 %all-gather.11.cloned.1.call-start = ((), (), s32[]{:S(2)}) async-start(), calls=%async_computation.8 | async-start | bytes 1327104 | tf_op jit(solution)/shard_map/all_gather | solution.py:185
  219.2 373.9 %all-reduce.13.cloned.1.call-start = ((), (), s32[]{:S(2)}) async-start(), calls=%async_computation.9 | async-start | bytes 9437184 | tf_op jit(solution)/shard_map/psum | solution.py:218
  228.3 585.8 %copy-start.45 = (f32[768]{0:T(1024)}, f32[768]{0:T(1024)S(1)}, u32[]{:S(2)}) copy-start(f32[768]{0:T(1024)S(1)} %get-tuple-element.396) | copy-start | bytes 9220
  393.4 420.7 %copy-start.41 = (f32[1536]{0:T(1024)}, f32[1536]{0:T(1024)S(1)}, u32[]{:S(2)}) copy-start(f32[1536]{0:T(1024)S(1)} %broadcast_multiply_fusion.3) | copy-start | bytes 18436
  393.9 420.1 %copy-start.43 = (f32[1536]{0:T(1024)}, f32[1536]{0:T(1024)S(1)}, u32[]{:S(2)}) copy-start(f32[1536]{0:T(1024)S(1)} %fusion.101) | copy-start | bytes 18436
  421.0 382.4 %all-reduce.15.cloned.1.call-start = ((), (), s32[]{:S(2)}) async-start(), calls=%async_computation.10 | async-start | bytes 9437184 | tf_op jit(solution)/shard_map/psum | solution.py:258
  617.5 185.9 %copy-start.47 = (f32[1536]{0:T(1024)}, f32[1536]{0:T(1024)S(1)}, u32[]{:S(2)}) copy-start(f32[1536]{0:T(1024)S(1)} %negate_multiply_fusion.1) | copy-start | bytes 18436
  633.2 530.8 %all-reduce.17.cloned.1.call-start = ((), (), s32[]{:S(2)}) async-start(), calls=%async_computation.11 | async-start | bytes 9437184 | tf_op jit(solution)/shard_map/psum | solution.py:283
  821.4 163.9 %copy-start.20 = (f32[1536,32]{0,1:T(8,128)S(1)}, f32[1536,32]{0,1:T(8,128)}, u32[]{:S(2)}) copy-start(f32[1536,32]{0,1:T(8,128)} %copy-done.19) | copy-start | bytes 589828
  992.9 383.2 %reduce-scatter.11.cloned.1.call-start = ((), (), s32[]{:S(2)}) async-start(), calls=%async_computation.12 | async-start | bytes 35168256 | tf_op jit(solution)/shard_map/reduce_scatter | solution.py:292
  1187.5 234.4 %reduce-scatter.17.cloned.1.call-start = ((), (), s32[]{:S(2)}) async-start(), calls=%async_computation.15 | async-start | bytes 2654208 | tf_op jit(solution)/shard_map/reduce_scatter | solution.py:296
  1194.9 264.7 %reduce-scatter.21.cloned.1.call-start = ((), (), s32[]{:S(2)}) async-start(), calls=%async_computation.20 | async-start | bytes 442368
  1196.0 302.0 %reduce-scatter.19.cloned.1.call-start = ((), (), s32[]{:S(2)}) async-start(), calls=%async_computation.19 | async-start | bytes 884736
  1201.7 354.7 %reduce-scatter.15.cloned.1.call-start = ((), (), s32[]{:S(2)}) async-start(), calls=%async_computation.14 | async-start | bytes 5308416 | tf_op jit(solution)/shard_map/reduce_scatter | solution.py:295
  1217.1 385.6 %reduce-scatter.13.cloned.1.call-start = ((), (), s32[]{:S(2)}) async-start(), calls=%async_computation.13 | async-start | bytes 2654208 | tf_op jit(solution)/shard_map/reduce_scatter | solution.py:293
  1224.7 586.4 %all-gather.13.cloned.1.call-start = ((), (), s32[]{:S(2)}) async-start(), calls=%async_computation.16 | async-start | bytes 14745600 | tf_op jit(solution)/shard_map/all_gather | solution.py:302
  1611.3 67.6 %copy-start.13 = (f32[96,2,768]{2,1,0:T(2,128)S(1)}, f32[96,2,768]{2,1,0:T(2,128)}, u32[]{:S(2)}) copy-start(f32[96,2,768]{2,1,0:T(2,128)} %param.37) | copy-start | bytes 1769476
  1611.3 67.6 %copy-start.14 = (f32[96,2,768]{2,0,1:T(8,128)S(1)}, f32[96,2,768]{2,0,1:T(8,128)}, u32[]{:S(2)}) copy-start(f32[96,2,768]{2,0,1:T(8,128)} %reduce-scatter.15.cloned.1.call-done) | copy-start | bytes 1769476
  1611.3 67.6 %copy-start.31 = (f32[96,2,768]{2,1,0:T(2,128)S(1)}, f32[96,2,768]{2,1,0:T(2,128)}, u32[]{:S(2)}) copy-start(f32[96,2,768]{2,1,0:T(2,128)} %param.43) | copy-start | bytes 1769476
  1611.3 67.6 %copy-start.32 = (f32[96,2,768]{2,1,0:T(2,128)S(1)}, f32[96,2,768]{2,1,0:T(2,128)}, u32[]{:S(2)}) copy-start(f32[96,2,768]{2,1,0:T(2,128)} %param.49) | copy-start | bytes 1769476
  1624.6 58.6 %copy-start.55 = (f32[2,96]{1,0:T(2,128)S(1)}, f32[2,96]{1,0:T(2,128)}, u32[]{:S(2)}) copy-start(f32[2,96]{1,0:T(2,128)} %param.45) | copy-start | bytes 2308
  1624.6 58.6 %copy-start.56 = (f32[2,96]{1,0:T(2,128)S(1)}, f32[2,96]{1,0:T(2,128)}, u32[]{:S(2)}) copy-start(f32[2,96]{1,0:T(2,128)} %param.51) | copy-start | bytes 2308
  1624.6 59.2 %copy-start.36 = (f32[192,96]{1,0:T(8,128)S(1)}, f32[192,96]{1,0:T(8,128)}, u32[]{:S(2)}) copy-start(f32[192,96]{1,0:T(8,128)} %param.36) | copy-start | bytes 221188
  1624.6 60.9 %copy-start.24 = (f32[768,96]{0,1:T(8,128)S(1)}, f32[768,96]{0,1:T(8,128)}, u32[]{:S(2)}) copy-start(f32[768,96]{0,1:T(8,128)} %param.38) | copy-start | bytes 884740
  1624.6 60.9 %copy-start.27 = (f32[768,96]{0,1:T(8,128)S(1)}, f32[768,96]{0,1:T(8,128)}, u32[]{:S(2)}) copy-start(f32[768,96]{0,1:T(8,128)} %reduce-scatter.17.cloned.1.call-done) | copy-start | bytes 884740
  1624.6 60.9 %copy-start.37 = (f32[768,96]{0,1:T(8,128)S(1)}, f32[768,96]{0,1:T(8,128)}, u32[]{:S(2)}) copy-start(f32[768,96]{0,1:T(8,128)} %param.44) | copy-start | bytes 884740
  (53 other events, 413.0 us)
Sparse Core Ops, SparseCore 0:
  22.9 71.4 all-gather.16
  125.0 50.4 all-gather.14
  178.0 27.8 all-gather.8
  218.6 170.7 all-reduce.10
  391.7 23.0 all-gather.10
  421.1 171.9 all-reduce.12
  633.3 170.0 all-reduce.14
  993.0 170.9 all-reduce.16
  1187.6 188.4 reduce-scatter.10
  1379.3 42.5 reduce-scatter.16
  1425.8 33.7 reduce-scatter.20
  1463.0 34.9 reduce-scatter.18
  1502.4 53.8 reduce-scatter.14
  1560.1 42.5 reduce-scatter.12
  1604.7 206.2 all-gather.12
where the time goes:
time: 1900 us
  waiting for transfers between devices  1240 us (65%)
  local copies, waits for them, and re-layouts  191 us (10%)
  matrix products  179 us (9%)
  other arithmetic  153 us (8%)
  blocking collectives  94.2 us (5%)
  between operations  21.7 us (1%)
    psum x1, waiting for transfers between devices, local(): lax.psum(jnp.dot(active_low, w_down, preferred_element_type=jnp.float32),...  171 us
    psum x1, waiting for transfers between devices, local(): lax.psum(contract(grad_qkv_low, w_qkv.reshape(D, -1), 1, 1), 'mp')  171 us
    psum x1, waiting for transfers between devices, local(): grad_one = grad_second + lax.psum(back_term, 'mp')  170 us
    psum x1, waiting for transfers between devices, local(): attn = lax.psum(attn_term, 'mp')  157 us
    reduce_scatter x1, waiting for transfers between devices, local(): lax.psum_scatter(grad_table, 'batch', scatter_dimension=0, tiled=True)  151 us
    all_gather x1, waiting for transfers between devices, local(): table_full = lax.all_gather(reduced[0], 'mp', axis=1, tiled=True)  123 us
    unnamed x132, local copies, waits for them, and re-layouts  102 us
    unnamed x17, waiting for transfers between devices  72.6 us
  transfers between devices with their start and end apart: 15, of which 14 were waited for; matrix products, arithmetic and copies ran while one was open for 8% of the time, Pallas kernels for 0%

commit v1 on v0

--- a/solution.py
+++ b/solution.py
@@ -207,7 +207,7 @@
     attended, log_totals = attend(query, keys, values, segment_ids, width)
     attended_low = attended.reshape(tokens, -1).astype(jnp.bfloat16)
     attn_term = jnp.dot(attended_low, w_out, preferred_element_type=jnp.float32)
-    attn = lax.psum(attn_term, "mp")
+    attn = jnp.sum(lax.all_gather(attn_term, "mp"), axis=0)
     hidden_one, first_back = jax.vjp(layer_norm, x_zero.astype(jnp.float32) + attn, gain[0])
     hidden_low = hidden_one.astype(jnp.bfloat16)
     gate_up = jnp.dot(hidden_low, w_gu.reshape(D, -1), preferred_element_type=jnp.float32).reshape(

time: 1900 us -> 2060 us (1.084)
  waiting for transfers between devices: 1240 us -> 1380 us
    all_gather x0 -> x1, waiting for transfers between devices: none -> 307 us  [local(): attn = jnp.sum(lax.all_gather(attn_term, 'mp'), axis=0)]
    psum x1 -> x0, waiting for transfers between devices: 157 us -> none  [local(): attn = lax.psum(attn_term, 'mp')]
  transfers between devices with their start and end apart: 15 -> 15, of which waited for: 14 -> 13; matrix products, arithmetic and copies ran while one was open for 8% -> 8% of each run, Pallas kernels for 0% -> 0%
where the time goes in v1:
time: 2060 us; the launch traced here: 2050 us
  waiting for transfers between devices  1380 us (67%)
  local copies, waits for them, and re-layouts  197 us (10%)
  matrix products  178 us (9%)
  other arithmetic  164 us (8%)
  blocking collectives  93.7 us (5%)
  between operations  21.6 us (1%)
    all_gather x1, waiting for transfers between devices, local(): attn = jnp.sum(lax.all_gather(attn_term, 'mp'), axis=0)  307 us
    psum x1, waiting for transfers between devices, local(): lax.psum(contract(grad_qkv_low, w_qkv.reshape(D, -1), 1, 1), 'mp')  171 us
    psum x1, waiting for transfers between devices, local(): grad_one = grad_second + lax.psum(back_term, 'mp')  170 us
    psum x1, waiting for transfers between devices, local(): lax.psum(jnp.dot(active_low, w_down, preferred_element_type=jnp.float32),...  169 us
    reduce_scatter x1, waiting for transfers between devices, local(): lax.psum_scatter(grad_table, 'batch', scatter_dimension=0, tiled=True)  151 us
    all_gather x1, waiting for transfers between devices, local(): table_full = lax.all_gather(reduced[0], 'mp', axis=1, tiled=True)  123 us
    unnamed x132, local copies, waits for them, and re-layouts  102 us
    unnamed x17, waiting for transfers between devices  72.6 us
  transfers between devices with their start and end apart: 15, of which 13 were waited for; matrix products, arithmetic and copies ran while one was open for 8% of the time, Pallas kernels for 0%

profile of v1, /device:TPU:0, one launch (start us, length us, event | category | flops | bytes accessed | tf_op | source)
XLA Modules:
  0.0 2053.6 jit_solution(3973925150874206368)
XLA Ops:
  7.3 12.4 copy.139
  31.4 63.1 %all-gather.21.cloned.1.call-done = bf16[8,3816,192]{1,2,0:T(8,128)(2,1)} async-done(((bf16[1,3816,192]{1,2,0:T(8,128)(2,1)}), bf16[8,3816,192]{1,2,0:T(8,128)(2,1)}) %all-gather.21.cloned.1.call-update) | async-done | bytes 11722768 | tf_op jit(solution)/shard_map/all_gather | solution.py:181
  94.5 18.1 copy.140
  112.6 11.2 gather_fusion.1
  126.6 13.2 all_gather.35
  151.5 24.0 %all-gather.17.cloned.1.call-done = bf16[1536,768]{0,1:T(8,128)(2,1)} async-done(((bf16[1536,192]{0,1:T(8,128)(2,1)}), bf16[1536,768]{0,1:T(8,128)(2,1)}) %all-gather.17.cloned.1.call-update) | async-done | bytes 2359312 | tf_op jit(solution)/shard_map/all_gather | solution.py:195
  179.8 33.9 %while.31 = (s32[]{:T(128)}, bf16[3,512,3,64]{1,3,2,0:T(8,128)(2,1)}, f32[3,3,512]{2,1,0:T(4,128)S(1)}, s32[3]{0:T(128)S(1)}, s32[1536]{0:T(1024)S(1)}, /*index=...) while((s32[]{:T(128)}, ...), condition=%wide.region_6.7_spmd, body=%wide.region_3.6_spmd.sunk | while | flops 633076224 | bytes 38029568 | solution.py:92
  233.1 307.0 %all-gather.19.cloned.1.call-done = f32[6144,768]{1,0:T(8,128)} async-done(((f32[1536,768]{1,0:T(8,128)}), f32[6144,768]{1,0:T(8,128)}) %all-gather.19.cloned.1.call-update) | async-done | bytes 18874384 | tf_op jit(solution)/shard_map/all_gather | solution.py:210
  540.1 10.4 reduce_sum.285
  581.9 169.5 %all-reduce.10.cloned.1.call-done = f32[1536,768]{0,1:T(8,128)} async-done(((f32[1536,768]{0,1:T(8,128)}), f32[1536,768]{0,1:T(8,128)}) %all-reduce.10.cloned.1.call-update) | async-done | bytes 4718608 | tf_op jit(solution)/shard_map/psum | solution.py:218
  791.5 169.9 %all-reduce.12.cloned.1.call-done = f32[1536,768]{0,1:T(8,128)} async-done(((f32[1536,768]{0,1:T(8,128)}), f32[1536,768]{0,1:T(8,128)}) %all-reduce.12.cloned.1.call-update) | async-done | bytes 4718608 | tf_op jit(solution)/shard_map/psum | solution.py:258
  979.4 161.7 %while.32 = (s32[]{:T(128)}, f32[1,1536,3,64]{1,3,2,0:T(8,128)}, f32[1,1536,3,64]{1,3,2,0:T(8,128)S(1)}, f32[3,512,3,64]{1,0,3,2:T(4,128)}, s32[3]{0:T(128)S(1)}...) while((s32[]{:T(128)}, f32[1,1536,3,64]{1,3,2,0:T(8,128)}, ...), condition=%wide.region_29.30_spmd.clone, body=%wide.region_26.29_spmd.clone.sunk | while | flops 1534130688 | bytes 86367704 | solution.py:137
  997.4 9.4 multiply_convert_fusion.4
  1051.1 9.4 multiply_convert_fusion.4
  1151.1 171.1 %all-reduce.14.cloned.1.call-done = f32[1536,768]{0,1:T(8,128)} async-done(((f32[1536,768]{0,1:T(8,128)}), f32[1536,768]{0,1:T(8,128)}) %all-reduce.14.cloned.1.call-update) | async-done | bytes 4718608 | tf_op jit(solution)/shard_map/psum | solution.py:283
  1324.4 21.2 %scatter_custom_fusion = f32[30528,192]{1,0:T(8,128)} fusion(s32[1536]{0:T(1024)} %copy-done.49, f32[1536,192]{1,0:T(8,128)S(1)} %copy.155, f32[]{:T(128)} %constant.228.clone.1), kind=kCustom, calls=%fused_computation.51 | custom fusion | flops 294912 | bytes 23446016 | tf_op jit(solution)/shard_map/scatter-add | solution.py:288
  1359.9 15.4 fusion.50
  1382.8 151.4 %reduce-scatter.11.cloned.1.call-done = f32[3816,192]{1,0:T(8,128)} async-done(((f32[30528,192]{1,0:T(8,128)}), f32[3816,192]{1,0:T(8,128)}) %reduce-scatter.11.cloned.1.call-update) | async-done | bytes 2930704 | tf_op jit(solution)/shard_map/reduce_scatter | solution.py:292
  1539.3 12.6 copy.158
  1551.9 28.0 %reduce-scatter.17.cloned.1.call-done = f32[768,96]{0,1:T(8,128)} async-done(((f32[768,768]{0,1:T(8,128)}), f32[768,96]{0,1:T(8,128)}) %reduce-scatter.17.cloned.1.call-update) | async-done | bytes 294928 | tf_op jit(solution)/shard_map/reduce_scatter | solution.py:296
  1581.6 36.1 %reduce-scatter.21.cloned.1.call-done = f32[96,2]{1,0:T(8,128)} async-done(((f32[768,2]{1,0:T(8,128)}), f32[96,2]{1,0:T(8,128)}) %reduce-scatter.21.cloned.1.call-update) | async-done | bytes 784
  1619.9 36.2 %reduce-scatter.19.cloned.1.call-done = f32[96,192]{1,0:T(8,128)} async-done(((f32[768,192]{1,0:T(8,128)}), f32[96,192]{1,0:T(8,128)}) %reduce-scatter.19.cloned.1.call-update) | async-done | bytes 73744
  1657.7 56.8 %reduce-scatter.15.cloned.1.call-done = f32[96,2,768]{2,0,1:T(8,128)} async-done(((f32[768,2,768]{2,0,1:T(8,128)}), f32[96,2,768]{2,0,1:T(8,128)}) %reduce-scatter.15.cloned.1.call-update) | async-done | bytes 589840 | tf_op jit(solution)/shard_map/reduce_scatter | solution.py:295
  1716.2 44.5 %reduce-scatter.13.cloned.1.call-done = f32[96,3,192]{2,0,1:T(8,128)} async-done(((f32[768,3,192]{2,0,1:T(8,128)}), f32[96,3,192]{2,0,1:T(8,128)}) %reduce-scatter.13.cloned.1.call-update) | async-done | bytes 221200 | tf_op jit(solution)/shard_map/reduce_scatter | solution.py:293
  1769.4 13.3 copy.156
  1782.7 53.5 %psum.31 = f32[]{:T(128)} all-reduce(f32[]{:T(128)S(6)} %add.322), channel_id=1, replica_groups=mesh['batch'=8,'mp'=4] {'batch','mp'}, use_global_device_ids=true, to_apply=%region_46.47 | all-reduce | flops 1 | bytes 8 | tf_op jit(solution)/shard_map/psum | solution.py:303
  1845.8 123.3 %all-gather.15.cloned.1.call-done = f32[3816,768]{0,1:T(8,128)} async-done(((f32[3816,192]{0,1:T(8,128)}), f32[3816,768]{0,1:T(8,128)}) %all-gather.15.cloned.1.call-update) | async-done | bytes 11722768 | tf_op jit(solution)/shard_map/all_gather | solution.py:302
  1969.1 17.3 fusion.46
  1986.5 12.3 copy.167
  1998.8 22.2 %fusion.45 = f32[3816,768]{0,1:T(8,128)} fusion(f32[3816,768]{0,1:T(8,128)} %copy.139, f32[3816,768]{0,1:T(8,128)} %get-tuple-element.440, f32[3816,768]{0,1:T(8,128)} %copy.156, f32[3816,768]{0,1:T(8,128)} %copy.158), kind=kLoop, calls=%fused_computation.57 | loop fusion | flops 41029632 | bytes 58613760 | tf_op jit(solution)/shard_map/sub | solution.py:147
  2021.0 12.3 copy.165
  2033.3 12.4 copy.169
  (349 shorter events, 358.5 us)
Async XLA Ops:
  7.2 87.3 %all-gather.21.cloned.1.call-start = ((), (), s32[]{:S(2)}) async-start(), calls=%async_computation.18 | async-start | bytes 13271040 | tf_op jit(solution)/shard_map/all_gather | solution.py:181
  22.8 152.7 %all-gather.17.cloned.1.call-start = ((), (), s32[]{:S(2)}) async-start(), calls=%async_computation.16 | async-start | bytes 2949120 | tf_op jit(solution)/shard_map/all_gather | solution.py:195
  31.4 81.2 %copy-start.49 = (s32[1536]{0:T(1024)}, s32[1536]{0:T(1024)S(1)}, u32[]{:S(2)}) copy-start(s32[1536]{0:T(1024)S(1)} %fusion.104) | copy-start | bytes 18436
  124.8 103.6 %all-gather.11.cloned.1.call-start = ((), (), s32[]{:S(2)}) async-start(), calls=%async_computation.6 | async-start | bytes 2654208 | tf_op jit(solution)/shard_map/all_gather | solution.py:184
  125.7 414.4 %all-gather.19.cloned.1.call-start = ((), (), s32[]{:S(2)}) async-start(), calls=%async_computation.17 | async-start | bytes 23592960 | tf_op jit(solution)/shard_map/all_gather | solution.py:210
  150.8 64.7 %copy-start.10 = (bf16[192,768]{0,1:T(8,128)(2,1)}, bf16[192,768]{0,1:T(8,128)(2,1)S(1)}, u32[]{:S(2)}) copy-start(bf16[192,768]{0,1:T(8,128)(2,1)S(1)} %all_gather.36) | copy-start | bytes 884740
  218.5 355.9 %all-gather.13.cloned.1.call-start = ((), (), s32[]{:S(2)}) async-start(), calls=%async_computation.7 | async-start | bytes 1327104 | tf_op jit(solution)/shard_map/all_gather | solution.py:185
  219.3 532.1 %all-reduce.10.cloned.1.call-start = ((), (), s32[]{:S(2)}) async-start(), calls=%async_computation.8 | async-start | bytes 9437184 | tf_op jit(solution)/shard_map/psum | solution.py:218
  228.4 743.7 %copy-start.45 = (f32[768]{0:T(1024)}, f32[768]{0:T(1024)S(1)}, u32[]{:S(2)}) copy-start(f32[768]{0:T(1024)S(1)} %get-tuple-element.396) | copy-start | bytes 9220
  560.7 411.4 %copy-start.41 = (f32[1536]{0:T(1024)}, f32[1536]{0:T(1024)S(1)}, u32[]{:S(2)}) copy-start(f32[1536]{0:T(1024)S(1)} %broadcast_multiply_fusion.3) | copy-start | bytes 18436
  561.3 410.8 %copy-start.43 = (f32[1536]{0:T(1024)}, f32[1536]{0:T(1024)S(1)}, u32[]{:S(2)}) copy-start(f32[1536]{0:T(1024)S(1)} %fusion.101) | copy-start | bytes 18436
  580.6 380.8 %all-reduce.12.cloned.1.call-start = ((), (), s32[]{:S(2)}) async-start(), calls=%async_computation.9 | async-start | bytes 9437184 | tf_op jit(solution)/shard_map/psum | solution.py:258
  775.6 185.9 %copy-start.47 = (f32[1536]{0:T(1024)}, f32[1536]{0:T(1024)S(1)}, u32[]{:S(2)}) copy-start(f32[1536]{0:T(1024)S(1)} %negate_multiply_fusion.1) | copy-start | bytes 18436
  791.3 530.9 %all-reduce.14.cloned.1.call-start = ((), (), s32[]{:S(2)}) async-start(), calls=%async_computation.10 | async-start | bytes 9437184 | tf_op jit(solution)/shard_map/psum | solution.py:283
  979.4 164.0 %copy-start.20 = (f32[1536,32]{0,1:T(8,128)S(1)}, f32[1536,32]{0,1:T(8,128)}, u32[]{:S(2)}) copy-start(f32[1536,32]{0,1:T(8,128)} %copy-done.19) | copy-start | bytes 589828
  1151.0 383.2 %reduce-scatter.11.cloned.1.call-start = ((), (), s32[]{:S(2)}) async-start(), calls=%async_computation.11 | async-start | bytes 35168256 | tf_op jit(solution)/shard_map/reduce_scatter | solution.py:292
  1345.6 234.3 %reduce-scatter.17.cloned.1.call-start = ((), (), s32[]{:S(2)}) async-start(), calls=%async_computation.14 | async-start | bytes 2654208 | tf_op jit(solution)/shard_map/reduce_scatter | solution.py:296
  1353.1 264.6 %reduce-scatter.21.cloned.1.call-start = ((), (), s32[]{:S(2)}) async-start(), calls=%async_computation.20 | async-start | bytes 442368
  1354.2 301.9 %reduce-scatter.19.cloned.1.call-start = ((), (), s32[]{:S(2)}) async-start(), calls=%async_computation.19 | async-start | bytes 884736
  1359.9 354.6 %reduce-scatter.15.cloned.1.call-start = ((), (), s32[]{:S(2)}) async-start(), calls=%async_computation.13 | async-start | bytes 5308416 | tf_op jit(solution)/shard_map/reduce_scatter | solution.py:295
  1375.4 385.3 %reduce-scatter.13.cloned.1.call-start = ((), (), s32[]{:S(2)}) async-start(), calls=%async_computation.12 | async-start | bytes 2654208 | tf_op jit(solution)/shard_map/reduce_scatter | solution.py:293
  1382.8 586.4 %all-gather.15.cloned.1.call-start = ((), (), s32[]{:S(2)}) async-start(), calls=%async_computation.15 | async-start | bytes 14745600 | tf_op jit(solution)/shard_map/all_gather | solution.py:302
  1769.3 67.6 %copy-start.13 = (f32[96,2,768]{2,1,0:T(2,128)S(1)}, f32[96,2,768]{2,1,0:T(2,128)}, u32[]{:S(2)}) copy-start(f32[96,2,768]{2,1,0:T(2,128)} %param.37) | copy-start | bytes 1769476
  1769.3 67.6 %copy-start.14 = (f32[96,2,768]{2,0,1:T(8,128)S(1)}, f32[96,2,768]{2,0,1:T(8,128)}, u32[]{:S(2)}) copy-start(f32[96,2,768]{2,0,1:T(8,128)} %reduce-scatter.15.cloned.1.call-done) | copy-start | bytes 1769476
  1769.3 67.6 %copy-start.31 = (f32[96,2,768]{2,1,0:T(2,128)S(1)}, f32[96,2,768]{2,1,0:T(2,128)}, u32[]{:S(2)}) copy-start(f32[96,2,768]{2,1,0:T(2,128)} %param.43) | copy-start | bytes 1769476
  1769.4 67.6 %copy-start.32 = (f32[96,2,768]{2,1,0:T(2,128)S(1)}, f32[96,2,768]{2,1,0:T(2,128)}, u32[]{:S(2)}) copy-start(f32[96,2,768]{2,1,0:T(2,128)} %param.49) | copy-start | bytes 1769476
  1782.7 58.6 %copy-start.55 = (f32[2,96]{1,0:T(2,128)S(1)}, f32[2,96]{1,0:T(2,128)}, u32[]{:S(2)}) copy-start(f32[2,96]{1,0:T(2,128)} %param.45) | copy-start | bytes 2308
  1782.7 58.6 %copy-start.56 = (f32[2,96]{1,0:T(2,128)S(1)}, f32[2,96]{1,0:T(2,128)}, u32[]{:S(2)}) copy-start(f32[2,96]{1,0:T(2,128)} %param.51) | copy-start | bytes 2308
  1782.7 59.2 %copy-start.36 = (f32[192,96]{1,0:T(8,128)S(1)}, f32[192,96]{1,0:T(8,128)}, u32[]{:S(2)}) copy-start(f32[192,96]{1,0:T(8,128)} %param.36) | copy-start | bytes 221188
  1782.7 60.9 %copy-start.24 = (f32[768,96]{0,1:T(8,128)S(1)}, f32[768,96]{0,1:T(8,128)}, u32[]{:S(2)}) copy-start(f32[768,96]{0,1:T(8,128)} %param.38) | copy-start | bytes 884740
  1782.7 60.9 %copy-start.27 = (f32[768,96]{0,1:T(8,128)S(1)}, f32[768,96]{0,1:T(8,128)}, u32[]{:S(2)}) copy-start(f32[768,96]{0,1:T(8,128)} %reduce-scatter.17.cloned.1.call-done) | copy-start | bytes 884740
  1782.7 60.9 %copy-start.37 = (f32[768,96]{0,1:T(8,128)S(1)}, f32[768,96]{0,1:T(8,128)}, u32[]{:S(2)}) copy-start(f32[768,96]{0,1:T(8,128)} %param.44) | copy-start | bytes 884740
  (53 other events, 417.6 us)
Sparse Core Ops, SparseCore 0:
  22.9 71.4 all-gather.20
  125.0 50.4 all-gather.16
  178.0 27.8 all-gather.10
  218.6 321.3 all-gather.18
  542.4 22.8 all-gather.12
  580.7 170.5 all-reduce.9
  791.4 170.0 all-reduce.11
  1151.1 170.9 all-reduce.13
  1345.7 188.4 reduce-scatter.10
  1537.4 42.4 reduce-scatter.16
  1583.9 33.8 reduce-scatter.20
  1621.1 34.9 reduce-scatter.18
  1660.5 53.9 reduce-scatter.14
  1718.2 42.4 reduce-scatter.12
  1762.8 206.3 all-gather.14
